TPU v7x, 32 devices: a whole 2x2x4 slice. The times are simulated.
32 devices in a mesh: req: 8 (over z, x), head: 4 (over y, core).
Axes of the slice: x: 2, y: 2, z: 4, core: 2. Of those that a mesh axis runs over, the one named last changes fastest.
Arguments:
- hidden_in: bfloat16 [64, 2048], P('req'), may hold values from -4 to 4
- queries: bfloat16 [64, 2048], P('req', 'head'), may hold values from -7.5 to 7.5
- new_keys: bfloat16 [64, 2048], P('req', 'head'), may hold values from -10 to 10
- new_values: bfloat16 [64, 2048], P('req', 'head'), may hold values from -8 to 8
- key_cache: bfloat16 [64, 1024, 2048], P('req', None, 'head'), may hold values from -4 to 4
- value_cache: bfloat16 [64, 1024, 2048], P('req', None, 'head'), may hold values from -6 to 6
- lengths: int32 [64], P('req'), may hold values from 2 to 1024, as said below
- out_proj: bfloat16 [2048, 2048], P('head'), may hold values from -0.5 to 0.5
- norm_gain: float32 [2048], replicated, may hold values from 0.1 to 1.9
- shared_gate: bfloat16 [5632, 2048], P(('req', 'head')), may hold values from -0.125 to 0.125
- shared_up: bfloat16 [5632, 2048], P(('req', 'head')), may hold values from -0.125 to 0.125
- shared_down: bfloat16 [5632, 2048], P(('req', 'head')), may hold values from -0.078125 to 0.078125
- shared_score: float32 [2048], replicated, may hold values from -0.125 to 0.125
- expert_gate: bfloat16 [8, 2048, 1408], P('req', None, 'head'), may hold values from -0.125 to 0.125
- expert_up: bfloat16 [8, 2048, 1408], P('req', None, 'head'), may hold values from -0.125 to 0.125
- expert_down: bfloat16 [8, 1408, 2048], P('req', 'head'), may hold values from -0.15625 to 0.15625
- expert_ids: int32 [64, 4], P('req'), may hold values from 0 to 7, all different within a row; in each aligned block of 8 rows (0 to 7, 8 to 15, ...) at most 8 rows name the same one
- route_weight: bfloat16 [64, 4], P('req'), may hold values from 0.099609375 to 0.59765625
Outputs:
- layer_out: bfloat16 [64, 2048], P('req')
Inputs may be any that keep to these rules, and one draw needn't show every extreme that they name: The first lengths[t] cache positions of request t are live; some request has exactly 1024. `expert_ids`: each row names 4 different experts. Among the 8 rows of one device (aligned blocks) no expert is named by more than 8 rows, and in some blocks one is named by exactly 8.
All inputs are finite; a program needn't handle non-finite values.
Results may differ from a plain program's by a relative error of at most 0.017.
Values may be sent and summed in bfloat16 or wider, within the bound.
A program may use at most 128 MiB of HBM per device.

v0:
```python
import jax
import jax.numpy as jnp
from jax import lax
from jax.sharding import PartitionSpec as P

HD = 128


EPSILON = 1e-06


def attend(queries, new_keys, new_values, key_cache, value_cache, lengths):
    row_count = queries.shape[0]
    head_count = queries.shape[1] // HD
    key_span = key_cache.shape[1]
    score_scale = HD ** (-0.5)
    query_heads = queries.reshape(row_count, head_count, HD)
    own_keys = new_keys.reshape(row_count, head_count, HD)
    own_values = new_values.reshape(row_count, head_count, HD)
    cache_keys = key_cache.reshape(row_count, key_span, head_count, HD)
    cache_values = value_cache.reshape(row_count, key_span, head_count, HD)
    scores = (
        jnp.einsum("bhd,blhd->bhl", query_heads, cache_keys, preferred_element_type=jnp.float32)
        * score_scale
    )
    own_score = (
        jnp.einsum("bhd,bhd->bh", query_heads, own_keys, preferred_element_type=jnp.float32)
        * score_scale
    )
    live_keys = jnp.arange(key_span, dtype=jnp.int32)[None, None, :] < lengths[:, None, None]
    highest = jnp.maximum(jnp.max(jnp.where(live_keys, scores, -1e30), axis=-1), own_score)
    weights = jnp.where(live_keys, jnp.exp(scores - highest[..., None]), 0.0)
    own_weight = jnp.exp(own_score - highest)
    totals = jnp.sum(weights, axis=-1) + own_weight
    probs = (weights / totals[..., None]).astype(jnp.bfloat16)
    own_prob = (own_weight / totals).astype(jnp.bfloat16)
    mixed = jnp.einsum("bhl,blhd->bhd", probs, cache_values, preferred_element_type=jnp.float32)
    mixed = mixed + own_prob.astype(jnp.float32)[..., None] * own_values.astype(jnp.float32)
    return mixed.astype(jnp.bfloat16).reshape(row_count, head_count * HD)


def normalize(residual, norm_gain):
    values = residual.astype(jnp.float32)
    mean_square = jnp.mean(values * values, axis=-1, keepdims=True)
    return (values * lax.rsqrt(mean_square + EPSILON) * norm_gain).astype(jnp.bfloat16)


def sender_slots(expert_ids, expert_count, capacity):
    flat_ids = expert_ids.reshape(-1)
    onehot_ids = (flat_ids[:, None] == jnp.arange(expert_count, dtype=jnp.int32)[None, :]).astype(
        jnp.int32
    )
    earlier = jnp.cumsum(onehot_ids, axis=0) - onehot_ids
    position = jnp.sum(earlier * onehot_ids, axis=1)
    return flat_ids * capacity + position


def per_device(
    hidden_in,
    queries,
    new_keys,
    new_values,
    key_cache,
    value_cache,
    lengths,
    out_proj,
    norm_gain,
    shared_gate,
    shared_up,
    shared_down,
    shared_score,
    expert_gate,
    expert_up,
    expert_down,
    expert_ids,
    route_weight,
):
    row_count = hidden_in.shape[0]
    model_width = hidden_in.shape[1]
    top_count = expert_ids.shape[1]
    owners = lax.axis_size("req")
    capacity = 8 * row_count // owners
    slot_count = owners * capacity
    attended = attend(queries, new_keys, new_values, key_cache, value_cache, lengths)
    partial_value = jnp.dot(attended, out_proj, preferred_element_type=jnp.float32)
    attn_out = lax.psum(partial_value, "head")
    residual = (hidden_in.astype(jnp.float32) + attn_out).astype(jnp.bfloat16)
    normed = normalize(residual, norm_gain)
    all_tokens = lax.all_gather(normed, "req", axis=0, tiled=True)
    targets = sender_slots(expert_ids, owners, capacity)
    placed = (jnp.arange(slot_count, dtype=jnp.int32)[:, None] == targets[None, :]).astype(
        jnp.float32
    )
    placed = placed.reshape(slot_count, row_count, top_count)
    dispatch = jnp.sum(placed, axis=2).astype(jnp.bfloat16)
    outgoing = jnp.dot(dispatch, normed, preferred_element_type=jnp.float32).astype(jnp.bfloat16)
    outgoing = outgoing.reshape(owners, capacity, model_width)
    block = lax.all_to_all(outgoing, "req", split_axis=0, concat_axis=0, tiled=True)
    sources = block.shape[0]
    items = block.shape[1]
    token_block = block.reshape(sources * items, model_width)
    gate = jnp.dot(token_block, expert_gate[0], preferred_element_type=jnp.float32)
    up_proj = jnp.dot(token_block, expert_up[0], preferred_element_type=jnp.float32)
    inner = (jax.nn.silu(gate) * up_proj).astype(jnp.bfloat16)
    result = jnp.dot(inner, expert_down[0], preferred_element_type=jnp.float32).reshape(
        sources, items, model_width
    )
    returned = lax.all_to_all(
        result.astype(jnp.bfloat16), "req", split_axis=0, concat_axis=0, tiled=True
    ).astype(result.dtype)
    combine = jnp.sum(placed * route_weight.astype(jnp.float32)[None, :, :], axis=2)
    routed_own = jnp.dot(
        combine.T, returned.reshape(slot_count, model_width), precision=lax.Precision.HIGHEST
    )
    blank = jnp.zeros((owners * row_count, model_width), jnp.float32)
    routed_all = lax.dynamic_update_slice_in_dim(
        blank, routed_own, lax.axis_index("req") * row_count, 0
    )
    contract = (((1,), (1,)), ((), ()))
    shared_g = lax.dot_general(
        all_tokens, shared_gate, contract, preferred_element_type=jnp.float32
    )
    shared_u = lax.dot_general(all_tokens, shared_up, contract, preferred_element_type=jnp.float32)
    shared_hidden = (jax.nn.silu(shared_g) * shared_u).astype(jnp.bfloat16)
    gate_all = jax.nn.sigmoid(
        jnp.dot(
            all_tokens,
            shared_score,
            preferred_element_type=jnp.float32,
            precision=lax.Precision.HIGHEST,
        )
    )
    term = (
        jnp.dot(shared_hidden, shared_down, preferred_element_type=jnp.float32) * gate_all[:, None]
    )
    summed = lax.psum_scatter(
        (term + routed_all).astype(jnp.bfloat16), "req", scatter_dimension=0, tiled=True
    )
    combined = lax.psum(summed, "head").astype(jnp.float32)
    return (residual.astype(jnp.float32) + combined).astype(jnp.bfloat16)


def solution(mesh):
    in_specs = (
        P("req", None),
        P("req", "head"),
        P("req", "head"),
        P("req", "head"),
        P("req", None, "head"),
        P("req", None, "head"),
        P("req"),
        P("head", None),
        P(),
        P(("req", "head"), None),
        P(("req", "head"), None),
        P(("req", "head"), None),
        P(),
        P("req", None, "head"),
        P("req", None, "head"),
        P("req", "head", None),
        P("req", None),
        P("req", None),
    )
    out_specs = P("req", None)
    return jax.shard_map(
        per_device, mesh=mesh, in_specs=in_specs, out_specs=out_specs, check_vma=False
    )
```

profile of v0, /device:TPU:0, one launch (start us, length us, event | category | flops | bytes accessed | tf_op | source)
XLA Modules:
  0.0 197.5 jit_solution(8394888308353872223)
XLA Ops:
  6.5 0.0 copy-start
  6.5 0.0 copy-start.9
  6.5 0.0 copy-start.2
  6.5 0.0 copy-start.6
  6.5 0.0 all-reduce.2.cloned.1.call-start
  6.6 11.6 %copy.41 = bf16[8,1024,512]{1,2,0:T(8,128)(2,1)} copy(bf16[8,1024,512]{2,1,0:T(8,128)(2,1)} %param.22) | data formatting | bytes 16777216 | tf_op jit(solution)/shard_map/reshape | solution.py:20
  18.2 0.0 copy-done.9
  18.2 0.1 iota_compare_fusion
  18.3 0.0 copy-done.2
  18.3 0.0 copy-done.6
  18.3 0.1 fusion.51
  18.4 0.0 copy-start.10
  18.4 4.7 %fusion.52 = f32[8,4,1,1024]{3,2,1,0:T(1,128)S(1)} fusion(bf16[8,1024,4,128]{1,3,2,0:T(8,128)(2,1)} %bitcast.98, bf16[8,4,128,1]{2,0,1,3:T(8,128)(2,1)S(1)} %bitcast.99), kind=kOutput, calls=%fused_computation.60 | convolution fusion | flops 8388608 | bytes 8527872 | tf_op jit(solution)/shard_map/bhd,blhd->bhl/dot_general | solution.py:23
  23.1 0.2 select_reduce_fusion
  23.3 0.2 fusion.36
  23.5 0.1 fusion.46
  23.6 0.5 copy-done.10
  24.2 0.0 copy-start.4
  24.2 1.2 fusion
  25.4 0.0 copy-start.7
  25.4 0.0 copy-start.8
  25.4 0.0 copy-start.3
  25.4 0.0 copy-start.5
  25.4 0.0 copy-start.1
  25.4 0.0 copy-done
  25.4 0.0 copy-done.4
  25.4 1.0 fusion.56
  26.5 0.0 all-reduce.2.cloned.1.call-update
  26.5 0.0 copy-done.7
  26.5 0.1 copy.29
  26.6 0.1 eq.30
  26.7 0.1 fusion.54
  26.7 0.1 reduce_window_sum.11
  26.8 0.2 select_reduce_fusion.2
  27.0 0.1 reduce_sum.50
  27.1 0.1 copy.31
  27.2 0.0 copy-done.8
  27.2 0.1 convert_reduce_fusion
  27.3 33.1 %all-reduce.2.cloned.1.call-done = f32[8,2048]{1,0:T(8,128)} async-done(((f32[8,2048]{1,0:T(8,128)}), f32[8,2048]{1,0:T(8,128)}) %all-reduce.2.cloned.1.call-update) | async-done | bytes 65552 | tf_op jit(solution)/shard_map/psum | solution.py:86
  60.4 0.0 copy-done.3
  60.4 1.0 fusion.37
  61.4 0.0 copy-done.5
  61.4 0.1 fusion.39
  61.5 1.0 fusion.3
  62.4 5.5 %all-to-all-start = ((bf16[8,8,2048]{2,1,0:T(8,128)(2,1)}), bf16[8,8,2048]{2,1,0:T(8,128)(2,1)S(1)}, u32[]{:S(2)}, u32[]{:S(2)}) async-start(bf16[8,8,2048]{2,1,0:T(8,128)(2,1)} %fusion.3), calls=%async_computation | async-start | bytes 524288 | tf_op jit(solution)/shard_map/all_to_all | solution.py:98
  67.9 32.5 %all_gather.3 = bf16[64,2048]{1,0:T(8,128)(2,1)S(1)} all-gather(bf16[8,2048]{1,0:T(8,128)(2,1)S(1)} %fusion.39), channel_id=1, replica_groups=mesh['req'=8,'head'=4] {'req'}, dimensions={0}, use_global_device_ids=true | all-gather | bytes 294912 | tf_op jit(solution)/shard_map/all_gather | solution.py:89
  100.4 0.0 copy-done.1
  100.4 0.4 fusion.65
  100.8 0.0 all-to-all-done
  100.8 1.9 fusion.8
  102.7 0.0 copy-start.11
  102.7 3.7 %convolution_convert_fusion = bf16[8,8,2048]{2,1,0:T(8,128)(2,1)} fusion(bf16[1,352,2048]{2,1,0:T(8,128)(2,1)} %param.33, bf16[1,2048,352]{1,2,0:T(8,128)(2,1)} %param.32, bf16[8,8,2048]{2,1,0:T(8,128)(2,1)S(1)} %all-to-all-done, f32[64,352]{1,0:T(8,128)S(1)} %fusion.8), kind=kOutput, calls=%fused_computation.4 | convolution fusion | flops 184815616 | bytes 3497984 | tf_op jit(solution)/shard_map/dot_general | solution.py:105
  106.4 4.5 %all-to-all-start.1 = ((bf16[8,8,2048]{2,1,0:T(8,128)(2,1)}), bf16[8,8,2048]{2,1,0:T(8,128)(2,1)S(1)}, u32[]{:S(2)}, u32[]{:S(2)}) async-start(bf16[8,8,2048]{2,1,0:T(8,128)(2,1)} %convolution_convert_fusion), calls=%async_computation.1 | async-start | bytes 524288 | tf_op jit(solution)/shard_map/all_to_all | solution.py:108
  110.9 0.0 reduce-scatter.2.cloned.1.call-start
  110.9 0.0 copy-done.11
  110.9 0.3 fusion.23
  111.2 2.1 %convolution_multiply_fusion = f32[64,2048]{1,0:T(8,128)S(1)} fusion(bf16[176,2048]{1,0:T(8,128)(2,1)} %param.29, bf16[64,2048]{1,0:T(8,128)(2,1)S(1)} %all_gather.3, bf16[176,2048]{1,0:T(8,128)(2,1)} %param.28, f32[64]{0:T(128)S(1)} %fusion.23, f32[64,176]{1,0:T(8,128)S(1)} %fusion.65), kind=kOutput, calls=%fused_computation.3 | convolution fusion | flops 92473344 | bytes 2273536 | tf_op jit(solution)/shard_map/dot_general | solution.py:134
  113.3 5.8 %all-to-all-done.1 = bf16[8,8,2048]{2,1,0:T(8,128)(2,1)S(1)} async-done(((bf16[8,8,2048]{2,1,0:T(8,128)(2,1)}), bf16[8,8,2048]{2,1,0:T(8,128)(2,1)S(1)}, u32[]{:S(2)}, u32[]{:S(2)}) %all-to-all-start.1) | async-done | bytes 262176 | tf_op jit(solution)/shard_map/all_to_all | solution.py:108
  119.1 0.2 fusion.4
  119.3 0.7 convert_element_type.84
  120.0 0.0 reduce-scatter.2.cloned.1.call-update
  120.1 59.2 %reduce-scatter.2.cloned.1.call-done = bf16[8,2048]{1,0:T(8,128)(2,1)} async-done(((bf16[64,2048]{1,0:T(8,128)(2,1)}), bf16[8,2048]{1,0:T(8,128)(2,1)}) %reduce-scatter.2.cloned.1.call-update) | async-done | bytes 32784 | tf_op jit(solution)/shard_map/reduce_scatter | solution.py:136
  179.2 10.8 %psum.15 = bf16[8,2048]{1,0:T(8,128)(2,1)S(1)} all-reduce(bf16[8,2048]{1,0:T(8,128)(2,1)} %reduce-scatter.2.cloned.1.call-done), channel_id=1, replica_groups=mesh['req'=8,'head'=4] {'head'}, use_global_device_ids=true, to_apply=%region_9.10 | all-reduce | flops 16384 | bytes 65536 | tf_op jit(solution)/shard_map/psum | solution.py:139
  190.0 0.6 fusion.40
  (5 shorter events, 0.0 us)
Async XLA Ops:
  6.5 18.9 %copy-start = (bf16[512,2048]{1,0:T(8,128)(2,1)S(1)}, bf16[512,2048]{1,0:T(8,128)(2,1)}, u32[]{:S(2)}) copy-start(bf16[512,2048]{1,0:T(8,128)(2,1)} %param.25) | copy-start | bytes 6291460
  6.5 11.7 %copy-start.9 = (s32[8]{0:T(128)S(1)}, s32[8]{0:T(128)}, u32[]{:S(2)}) copy-start(s32[8]{0:T(128)} %param.24) | copy-start | bytes 100
  6.5 11.8 %copy-start.2 = (bf16[8,512]{1,0:T(8,128)(2,1)S(1)}, bf16[8,512]{1,0:T(8,128)(2,1)}, u32[]{:S(2)}) copy-start(bf16[8,512]{1,0:T(8,128)(2,1)} %param.19) | copy-start | bytes 24580
  6.5 11.8 %copy-start.6 = (bf16[8,512]{1,0:T(8,128)(2,1)S(1)}, bf16[8,512]{1,0:T(8,128)(2,1)}, u32[]{:S(2)}) copy-start(bf16[8,512]{1,0:T(8,128)(2,1)} %param.20) | copy-start | bytes 24580
  6.5 53.9 %all-reduce.2.cloned.1.call-start = ((), (), s32[]{:S(2)}) async-start(), calls=%async_computation.3 | async-start | bytes 131072 | tf_op jit(solution)/shard_map/psum | solution.py:86
  18.4 5.8 %copy-start.10 = (bf16[8,1024,512]{2,1,0:T(8,128)(2,1)S(1)}, bf16[8,1024,512]{2,1,0:T(8,128)(2,1)}, u32[]{:S(2)}) copy-start(bf16[8,1024,512]{2,1,0:T(8,128)(2,1)} %param.23) | copy-start | bytes 25165828
  24.2 1.3 copy-start.4
  25.4 1.1 copy-start.7
  25.4 1.8 copy-start.8
  25.4 35.0 %copy-start.3 = (bf16[8,2048]{1,0:T(8,128)(2,1)S(1)}, bf16[8,2048]{1,0:T(8,128)(2,1)}, u32[]{:S(2)}) copy-start(bf16[8,2048]{1,0:T(8,128)(2,1)} %param.18) | copy-start | bytes 98308
  25.4 36.0 %copy-start.5 = (f32[2048]{0:T(1024)S(1)}, f32[2048]{0:T(1024)}, u32[]{:S(2)}) copy-start(f32[2048]{0:T(1024)} %param.26) | copy-start | bytes 24580
  25.4 75.0 %copy-start.1 = (bf16[176,2048]{1,0:T(8,128)(2,1)S(1)}, bf16[176,2048]{1,0:T(8,128)(2,1)}, u32[]{:S(2)}) copy-start(bf16[176,2048]{1,0:T(8,128)(2,1)} %param.27) | copy-start | bytes 2162692
  62.4 38.3 %all-to-all-start = ((bf16[8,8,2048]{2,1,0:T(8,128)(2,1)}), bf16[8,8,2048]{2,1,0:T(8,128)(2,1)S(1)}, u32[]{:S(2)}, u32[]{:S(2)}) async-start(bf16[8,8,2048]{2,1,0:T(8,128)(2,1)} %fusion.3), calls=%async_computation | async-start | bytes 524288 | tf_op jit(solution)/shard_map/all_to_all | solution.py:98
  102.7 8.2 %copy-start.11 = (f32[2048]{0:T(1024)S(1)}, f32[2048]{0:T(1024)}, u32[]{:S(2)}) copy-start(f32[2048]{0:T(1024)} %param.30) | copy-start | bytes 24580
  106.4 12.7 %all-to-all-start.1 = ((bf16[8,8,2048]{2,1,0:T(8,128)(2,1)}), bf16[8,8,2048]{2,1,0:T(8,128)(2,1)S(1)}, u32[]{:S(2)}, u32[]{:S(2)}) async-start(bf16[8,8,2048]{2,1,0:T(8,128)(2,1)} %convolution_convert_fusion), calls=%async_computation.1 | async-start | bytes 524288 | tf_op jit(solution)/shard_map/all_to_all | solution.py:108
  110.9 68.4 %reduce-scatter.2.cloned.1.call-start = ((), (), s32[]{:S(2)}) async-start(), calls=%async_computation.4 | async-start | bytes 294912 | tf_op jit(solution)/shard_map/reduce_scatter | solution.py:136
Sparse Core Ops, SparseCore 0:
  26.6 33.7 all-reduce.1
  120.2 59.0 reduce-scatter.1
where the time goes:
time: 198 us
  waiting for transfers between devices  98.1 us (50%)
  blocking collectives  43.2 us (22%)
  matrix products  16.5 us (8%)
  between operations  13.6 us (7%)
  local copies, waits for them, and re-layouts  12.5 us (6%)
  starting transfers between devices  10.1 us (5%)
  other arithmetic  3.49 us (2%)
    reduce_scatter x1, waiting for transfers between devices, per_device(): lax.psum_scatter((term + routed_all).astype(jnp.bfloat16), 'req', scatter...  59.2 us
    psum x1, waiting for transfers between devices, per_device(): attn_out = lax.psum(partial_value, 'head')  33.1 us
    all_gather x1, blocking collectives, per_device(): all_tokens = lax.all_gather(normed, 'req', axis=0, tiled=True)  32.5 us
    reshape x1, local copies, waits for them, and re-layouts, attend(): cache_keys = key_cache.reshape(row_count, key_span, head_count, HD)  11.6 us
    psum x1, blocking collectives, per_device(): combined = lax.psum(summed, 'head').astype(jnp.float32)  10.8 us
    all_to_all x1, waiting for transfers between devices, per_device(): lax.all_to_all(result.astype(jnp.bfloat16), 'req', split_axis=0, concat_a...  5.78 us
    all_to_all x1, starting transfers between devices, per_device(): lax.all_to_all(outgoing, 'req', split_axis=0, concat_axis=0, tiled=True)  5.51 us
    dot_general x1, matrix products, attend(): jnp.einsum('bhd,blhd->bhl', query_heads, cache_keys, preferred_element_ty...  4.72 us
  transfers between devices with their start and end apart: 4, of which 3 were waited for; matrix products, arithmetic and copies ran while one was open for 2% of the time, Pallas kernels for 0%

commit v1 on v0

v1 whole, which is shorter than its diff:
```python
import functools

import jax
import jax.numpy as jnp
from jax import lax
from jax.experimental import pallas as pl
from jax.experimental.pallas import tpu as pltpu
from jax.sharding import PartitionSpec as P

HD = 128
EPSILON = 1e-06
CHUNK = 256
MESH = pl.DeviceIdType.MESH


def attend_kernel(
    lengths_ref, q_ref, nk_ref, nv_ref, k_hbm, v_hbm, proj_hbm, out_ref,
    k_buf, v_buf, proj_buf, attended, k_sem, v_sem, proj_sem,
):
    rows, span, width = k_buf.shape
    heads = width // HD
    chunks = span // CHUNK
    scale = HD ** (-0.5)

    def k_copy(b, c):
        part = pl.ds(c * CHUNK, CHUNK)
        return pltpu.make_async_copy(k_hbm.at[b, part], k_buf.at[b, part], k_sem.at[b, c])

    def v_copy(b, c):
        part = pl.ds(c * CHUNK, CHUNK)
        return pltpu.make_async_copy(v_hbm.at[b, part], v_buf.at[b, part], v_sem.at[b, c])

    def live(b, c):
        return lengths_ref[b] > c * CHUNK

    for copy in (k_copy, v_copy):
        for b in range(rows):
            for c in range(chunks):
                @pl.when(live(b, c))
                def _():
                    copy(b, c).start()
    proj_copy = pltpu.make_async_copy(proj_hbm, proj_buf, proj_sem)
    proj_copy.start()
    for b in range(rows):
        for c in range(1, chunks):
            @pl.when(jnp.logical_not(live(b, c)))
            def _():
                v_buf[b, c * CHUNK:(c + 1) * CHUNK, :] = jnp.zeros((CHUNK, width), v_buf.dtype)
    for b in range(rows):
        for c in range(chunks):
            @pl.when(live(b, c))
            def _():
                k_copy(b, c).wait()

    group = max(8, heads)
    row_id = lax.broadcasted_iota(jnp.int32, (group, width), 0)
    lane_head = lax.broadcasted_iota(jnp.int32, (group, width), 1) // HD
    own_head = row_id == lane_head
    position = lax.broadcasted_iota(jnp.int32, (group, span), 1)
    queries = q_ref[...].astype(jnp.float32)
    own_keys = nk_ref[...].astype(jnp.float32)
    own_values = nv_ref[...].astype(jnp.float32)
    probs = []
    own_probs = []
    for b in range(rows):
        spread = jnp.where(own_head, queries[b:b + 1, :], 0.0)
        scores = lax.dot_general(
            spread.astype(jnp.bfloat16), k_buf[b], (((1,), (1,)), ((), ())),
            preferred_element_type=jnp.float32,
        ) * scale
        own_score = jnp.sum(spread * own_keys[b:b + 1, :], axis=1, keepdims=True) * scale
        alive = position < lengths_ref[b]
        scores = jnp.where(alive, scores, -1e30)
        highest = jnp.maximum(jnp.max(scores, axis=1, keepdims=True), own_score)
        weights = jnp.where(alive, jnp.exp(scores - highest), 0.0)
        own_weight = jnp.exp(own_score - highest)
        total = jnp.sum(weights, axis=1, keepdims=True) + own_weight
        probs.append((weights / total).astype(jnp.bfloat16))
        own_probs.append((own_weight / total).astype(jnp.bfloat16).astype(jnp.float32))
    for b in range(rows):
        for c in range(chunks):
            @pl.when(live(b, c))
            def _():
                v_copy(b, c).wait()
    for b in range(rows):
        mixed = jnp.dot(probs[b], v_buf[b], preferred_element_type=jnp.float32)
        mixed = mixed + own_probs[b] * own_values[b:b + 1, :]
        attended[b:b + 1, :] = jnp.sum(jnp.where(own_head, mixed, 0.0), axis=0, keepdims=True)
    proj_copy.wait()
    out_ref[...] = jnp.dot(
        attended[...].astype(jnp.bfloat16), proj_buf[...], preferred_element_type=jnp.float32
    )


def silu(x):
    return x / (1.0 + jnp.exp(-x))


def expert_kernel(
    req_count, head_count,
    part_ref, hid_ref, gain_ref, score_ref, ids_ref, rw_ref,
    sg_hbm, su_hbm, sd_hbm, eg_hbm, eu_hbm, ed_hbm,
    out_ref,
    sg, su, sd, eg, eu, ed, weight_sems,
    w_all, terms1, resid_all, send5, terms5, total6, send6, terms6, final,
    w_send, w_recv, s1, r1, s2, r2, s3, r3, s5, r5, s6, r6, s7, r7,
):
    rows, model = hid_ref.shape
    cols = model // head_count
    tokens = req_count * rows
    me_r = lax.axis_index("req")
    me_h = lax.axis_index("head")

    loads = [
        pltpu.make_async_copy(src, dst, weight_sems.at[i])
        for i, (src, dst) in enumerate((
            (eg_hbm.at[0], eg), (eu_hbm.at[0], eu), (sg_hbm, sg), (su_hbm, su),
            (sd_hbm, sd), (ed_hbm.at[0], ed),
        ))
    ]
    for load in loads:
        load.start()

    def req_peer(d):
        return lax.rem(me_r + d, req_count)

    def req_source(d):
        return lax.rem(me_r + (req_count - d), req_count)

    def head_peer(d):
        return lax.rem(me_h + d, head_count)

    def head_source(d):
        return lax.rem(me_h + (head_count - d), head_count)

    def remote(src, dst, send, recv, r, h):
        return pltpu.make_async_remote_copy(
            src_ref=src, dst_ref=dst, send_sem=send, recv_sem=recv,
            device_id=(r, h), device_id_type=MESH,
        )

    barrier = pltpu.get_barrier_semaphore()
    for d in range(1, head_count):
        pl.semaphore_signal(barrier, inc=1, device_id=(me_r, head_peer(d)), device_id_type=MESH)
    for d in range(1, req_count):
        pl.semaphore_signal(barrier, inc=1, device_id=(req_peer(d), me_h), device_id_type=MESH)
    lane = lax.broadcasted_iota(jnp.int32, (rows, 128), 1)
    table = jnp.zeros((rows, 128), jnp.float32)
    route = rw_ref[...].astype(jnp.float32)
    ids = ids_ref[...]
    for k in range(ids.shape[1]):
        table = table + jnp.where(ids[:, k:k + 1] == lane, route[:, k:k + 1], 0.0)
    w_all[me_r] = table
    pl.semaphore_wait(barrier, head_count + req_count - 2)

    def my_cols(h):
        return pl.ds(pl.multiple_of(h * cols, 128), cols)

    sends = []

    def start(copy):
        copy.start()
        sends.append(copy)

    for d in range(1, head_count):
        start(remote(
            part_ref.at[:, my_cols(head_peer(d))], terms1.at[d], s1.at[d], r1.at[d],
            me_r, head_peer(d),
        ))
    for d in range(1, req_count):
        start(remote(
            w_all.at[me_r], w_all.at[me_r], w_send.at[d], w_recv.at[d], req_peer(d), me_h,
        ))
    summed = part_ref[:, my_cols(me_h)]
    for d in range(1, head_count):
        remote(
            part_ref.at[:, my_cols(me_h)], terms1.at[d], s1.at[d], r1.at[d], me_r, head_peer(d),
        ).wait_recv()
        summed = summed + terms1[d]
    resid = (hid_ref[:, my_cols(me_h)].astype(jnp.float32) + summed).astype(jnp.bfloat16)
    resid_all[me_h, me_r] = resid

    for d in range(1, req_count):
        block = resid_all.at[me_h, me_r]
        start(remote(block, block, s2.at[d], r2.at[d], req_peer(d), me_h))
    for j in range(req_count):
        block = resid_all.at[me_h, req_source(j)]
        if j > 0:
            remote(block, block, s2.at[j], r2.at[j], req_peer(j), me_h).wait_recv()
        for d in range(1, head_count):
            start(remote(block, block, s3.at[d, j], r3.at[d, j], me_r, head_peer(d)))
    for j in range(req_count):
        for d in range(1, head_count):
            block = resid_all.at[head_source(d), req_source(j)]
            remote(block, block, s3.at[d, j], r3.at[d, j], me_r, head_peer(d)).wait_recv()

    wide = [
        resid_all[h].astype(jnp.float32).reshape(tokens, cols) for h in range(head_count)
    ]
    square = jnp.sum(wide[0] * wide[0], axis=1, keepdims=True)
    for h in range(1, head_count):
        square = square + jnp.sum(wide[h] * wide[h], axis=1, keepdims=True)
    inverse = lax.rsqrt(square / model + EPSILON)
    normed = [
        (wide[h] * inverse * gain_ref[:, h * cols:(h + 1) * cols]).astype(jnp.bfloat16)
        for h in range(head_count)
    ]
    logit = jnp.zeros((tokens, 1), jnp.float32)
    for h in range(head_count):
        logit = logit + jnp.sum(
            normed[h].astype(jnp.float32) * score_ref[:, h * cols:(h + 1) * cols],
            axis=1, keepdims=True,
        )
    gate_scale = 1.0 / (1.0 + jnp.exp(-logit))
    for load in loads:
        load.wait()

    def project(weight):
        out = None
        for h in range(head_count):
            term = jnp.dot(
                normed[h], weight[h * cols:(h + 1) * cols, :], preferred_element_type=jnp.float32
            )
            out = term if out is None else out + term
        return out

    def project_t(weight):
        out = None
        for h in range(head_count):
            term = lax.dot_general(
                normed[h], weight[:, h * cols:(h + 1) * cols], (((1,), (1,)), ((), ())),
                preferred_element_type=jnp.float32,
            )
            out = term if out is None else out + term
        return out

    inner = (silu(project(eg)) * project(eu)).astype(jnp.bfloat16)
    shared = (silu(project_t(sg)) * project_t(su)).astype(jnp.bfloat16)
    for d in range(1, req_count):
        block = w_all.at[req_source(d)]
        remote(block, block, w_send.at[d], w_recv.at[d], req_peer(d), me_h).wait_recv()
    weights = w_all[...].reshape(tokens, 128)
    wide_lane = lax.broadcasted_iota(jnp.int32, (tokens, 128), 1)
    weight = jnp.sum(jnp.where(wide_lane == me_r, weights, 0.0), axis=1, keepdims=True)

    def column_terms(h):
        part = my_cols(h)
        term = gate_scale * jnp.dot(shared, sd[:, part], preferred_element_type=jnp.float32)
        term = term + weight * jnp.dot(inner, ed[:, part], preferred_element_type=jnp.float32)
        return term.reshape(req_count, rows, cols)

    for d in range(1, head_count):
        send5[d] = column_terms(head_peer(d)).astype(jnp.bfloat16)
        start(remote(send5.at[d], terms5.at[d], s5.at[d], r5.at[d], me_r, head_peer(d)))
    total = column_terms(me_h)
    for d in range(1, head_count):
        remote(
            send5.at[d], terms5.at[d], s5.at[d], r5.at[d], me_r, head_peer(d)
        ).wait_recv()
        total = total + terms5[d].astype(jnp.float32)
    total6[...] = total
    send6[...] = total.astype(jnp.bfloat16)
    for d in range(1, req_count):
        start(remote(
            send6.at[req_peer(d)], terms6.at[d], s6.at[d], r6.at[d], req_peer(d), me_h
        ))
    combined = total6[me_r]
    for d in range(1, req_count):
        remote(
            send6.at[req_peer(d)], terms6.at[d], s6.at[d], r6.at[d], req_peer(d), me_h
        ).wait_recv()
        combined = combined + terms6[d].astype(jnp.float32)
    final[me_h] = (resid.astype(jnp.float32) + combined).astype(jnp.bfloat16)
    for d in range(1, head_count):
        start(remote(
            final.at[me_h], final.at[me_h], s7.at[d], r7.at[d], me_r, head_peer(d)
        ))
    for d in range(1, head_count):
        block = final.at[head_source(d)]
        remote(block, block, s7.at[d], r7.at[d], me_r, head_peer(d)).wait_recv()
    for h in range(head_count):
        out_ref[:, h * cols:(h + 1) * cols] = final[h]
    for copy in sends:
        copy.wait_send()


VMEM_SPEC = pl.BlockSpec(memory_space=pltpu.VMEM)
ANY_SPEC = pl.BlockSpec(memory_space=pl.ANY)


def per_device(
    req_count, head_count,
    hidden_in, queries, new_keys, new_values, key_cache, value_cache, lengths, out_proj,
    norm_gain, shared_gate, shared_up, shared_down, shared_score, expert_gate, expert_up,
    expert_down, expert_ids, route_weight,
):
    rows, model = hidden_in.shape
    span, width = key_cache.shape[1:]
    bf16, f32 = jnp.bfloat16, jnp.float32
    dma = pltpu.SemaphoreType.DMA
    chunks = span // CHUNK
    partial = pl.pallas_call(
        attend_kernel,
        out_shape=jax.ShapeDtypeStruct((rows, model), f32),
        in_specs=[pl.BlockSpec(memory_space=pltpu.SMEM)] + [VMEM_SPEC] * 3 + [ANY_SPEC] * 3,
        out_specs=VMEM_SPEC,
        scratch_shapes=[
            pltpu.VMEM((rows, span, width), bf16),
            pltpu.VMEM((rows, span, width), bf16),
            pltpu.VMEM(out_proj.shape, bf16),
            pltpu.VMEM((rows, width), f32),
            dma((rows, chunks)), dma((rows, chunks)), dma,
        ],
        compiler_params=pltpu.CompilerParams(vmem_limit_bytes=40 << 20),
        name="attend",
    )(lengths, queries, new_keys, new_values, key_cache, value_cache, out_proj)

    cols = model // head_count
    return pl.pallas_call(
        functools.partial(expert_kernel, req_count, head_count),
        out_shape=jax.ShapeDtypeStruct((rows, model), bf16),
        in_specs=[VMEM_SPEC] * 6 + [ANY_SPEC] * 6,
        out_specs=VMEM_SPEC,
        scratch_shapes=[
            pltpu.VMEM(shared_gate.shape, bf16),
            pltpu.VMEM(shared_up.shape, bf16),
            pltpu.VMEM(shared_down.shape, bf16),
            pltpu.VMEM(expert_gate.shape[1:], bf16),
            pltpu.VMEM(expert_up.shape[1:], bf16),
            pltpu.VMEM(expert_down.shape[1:], bf16),
            dma((6,)),
            pltpu.VMEM((req_count, rows, 128), f32),
            pltpu.VMEM((head_count, rows, cols), f32),
            pltpu.VMEM((head_count, req_count, rows, cols), bf16),
            pltpu.VMEM((head_count, req_count, rows, cols), bf16),
            pltpu.VMEM((head_count, req_count, rows, cols), bf16),
            pltpu.VMEM((req_count, rows, cols), f32),
            pltpu.VMEM((req_count, rows, cols), bf16),
            pltpu.VMEM((req_count, rows, cols), bf16),
            pltpu.VMEM((head_count, rows, cols), bf16),
            dma((req_count,)), dma((req_count,)),
            dma((head_count,)), dma((head_count,)),
            dma((req_count,)), dma((req_count,)),
            dma((head_count, req_count)), dma((head_count, req_count)),
            dma((head_count,)), dma((head_count,)),
            dma((req_count,)), dma((req_count,)),
            dma((head_count,)), dma((head_count,)),
        ],
        compiler_params=pltpu.CompilerParams(
            vmem_limit_bytes=40 << 20, collective_id=0, has_side_effects=True
        ),
        name="experts",
    )(
        partial, hidden_in, norm_gain.reshape(1, model), shared_score.reshape(1, model),
        expert_ids, route_weight,
        shared_gate, shared_up, shared_down, expert_gate, expert_up, expert_down,
    )


def solution(mesh):
    in_specs = (
        P("req", None),
        P("req", "head"),
        P("req", "head"),
        P("req", "head"),
        P("req", None, "head"),
        P("req", None, "head"),
        P("req"),
        P("head", None),
        P(),
        P(("req", "head"), None),
        P(("req", "head"), None),
        P(("req", "head"), None),
        P(),
        P("req", None, "head"),
        P("req", None, "head"),
        P("req", "head", None),
        P("req", None),
        P("req", None),
    )
    body = functools.partial(per_device, mesh.shape["req"], mesh.shape["head"])
    return jax.shard_map(
        body, mesh=mesh, in_specs=in_specs, out_specs=P("req", None), check_vma=False
    )
```

time: 198 us -> 55.4 us (0.28)
  waiting for transfers between devices: 98.1 us -> 0 us
  blocking collectives: 43.2 us -> 0 us
  Pallas kernels: 0 us -> 37.5 us
  matrix products: 16.5 us -> 0 us
  between operations: 13.6 us -> 0.11 us
  starting transfers between devices: 10.1 us -> 0 us
  local copies, waits for them, and re-layouts: 12.5 us -> 17.3 us
  other arithmetic: 3.49 us -> 0 us
    reduce_scatter x1 -> x0, waiting for transfers between devices: 59.2 us -> none  [per_device(): lax.psum_scatter((term + routed_all).astype(jnp.bfloat16), 'req', scatter...]
    pallas_call x0 -> x2, Pallas kernels: none -> 37.5 us  [the longest x1 31 us: per_device(): pl.pallas_call(functools.partial(expert_kernel, req_count, head_count), o...]
    psum x1 -> x0, waiting for transfers between devices: 33.1 us -> none  [per_device(): attn_out = lax.psum(partial_value, 'head')]
    all_gather x1 -> x0, blocking collectives: 32.5 us -> none  [per_device(): all_tokens = lax.all_gather(normed, 'req', axis=0, tiled=True)]
    unnamed x25 -> x33, local copies, waits for them, and re-layouts: 0.67 us -> 17.3 us
    dot_general x10 -> x0, matrix products: 16.5 us -> none  [the longest x1 4.72 us: attend(): jnp.einsum('bhd,blhd->bhl', query_heads, cache_keys, preferred_element_ty...]
    reshape x1 -> x0, local copies, waits for them, and re-layouts: 11.6 us -> none  [attend(): cache_keys = key_cache.reshape(row_count, key_span, head_count, HD)]
    psum x1 -> x0, blocking collectives: 10.8 us -> none  [per_device(): combined = lax.psum(summed, 'head').astype(jnp.float32)]
  transfers between devices with their start and end apart: 4 -> 0, of which waited for: 3 -> 0; matrix products, arithmetic and copies ran while one was open for 2% -> 0% of each run, Pallas kernels for 0% -> 0%
where the time goes in v1:
time: 55.4 us; the launch traced here: 54.9 us
  Pallas kernels  37.5 us (68%)
  local copies, waits for them, and re-layouts  17.3 us (31%)
    pallas_call x1, Pallas kernels, per_device(): pl.pallas_call(functools.partial(expert_kernel, req_count, head_count), o...  31 us
    unnamed x33, local copies, waits for them, and re-layouts  17.3 us
    pallas_call x1, Pallas kernels, per_device(): pl.pallas_call(attend_kernel, out_shape=jax.ShapeDtypeStruct((rows, model...  6.55 us

profile of v1, /device:TPU:0, one launch (start us, length us, event | category | flops | bytes accessed | tf_op | source)
XLA Modules:
  0.0 54.9 jit_solution(11035301541808895292)
XLA Ops:
  0.0 0.8 %copy.20.rw_ref = bf16[8,4]{1,0:T(8,128)(2,1)S(1)} copy(bf16[8,4]{0,1:T(4,128)(2,1)} %param.35) | data formatting | bytes 128 | tf_op args[17]
  0.8 0.8 %copy.19.ids_ref = s32[8,4]{1,0:T(8,128)S(1)} copy(s32[8,4]{0,1:T(4,128)} %param.34) | data formatting | bytes 256 | tf_op args[16]
  1.5 0.0 copy-start
  1.5 3.4 %copy-done = bf16[8,1024,512]{2,1,0:T(8,128)(2,1)S(1)} copy-done((bf16[8,1024,512]{2,1,0:T(8,128)(2,1)S(1)}, bf16[8,1024,512]{2,1,0:T(8,128)(2,1)}, u32[]{:S(2)}) %copy-start) | copy-done | bytes 8388632
  4.9 0.0 copy-start.1
  4.9 1.6 %copy-done.1 = bf16[512,2048]{1,0:T(8,128)(2,1)S(1)} copy-done((bf16[512,2048]{1,0:T(8,128)(2,1)S(1)}, bf16[512,2048]{1,0:T(8,128)(2,1)}, u32[]{:S(2)}) %copy-start.1) | copy-done | bytes 2097176
  6.5 0.0 copy-start.7
  6.5 0.7 %copy-done.7 = bf16[8,512]{1,0:T(8,128)(2,1)S(1)} copy-done((bf16[8,512]{1,0:T(8,128)(2,1)S(1)}, bf16[8,512]{1,0:T(8,128)(2,1)}, u32[]{:S(2)}) %copy-start.7) | copy-done | bytes 8216
  7.2 0.0 copy-start.8
  7.2 0.7 %copy-done.8 = bf16[8,512]{1,0:T(8,128)(2,1)S(1)} copy-done((bf16[8,512]{1,0:T(8,128)(2,1)S(1)}, bf16[8,512]{1,0:T(8,128)(2,1)}, u32[]{:S(2)}) %copy-start.8) | copy-done | bytes 8216
  7.9 0.0 copy-start.9
  7.9 0.7 %copy-done.9 = bf16[8,512]{1,0:T(8,128)(2,1)S(1)} copy-done((bf16[8,512]{1,0:T(8,128)(2,1)S(1)}, bf16[8,512]{1,0:T(8,128)(2,1)}, u32[]{:S(2)}) %copy-start.9) | copy-done | bytes 8216
  8.6 0.0 copy-start.12
  8.6 0.7 %copy-done.12 = s32[8]{0:T(128)S(1)} copy-done((s32[8]{0:T(128)S(1)}, s32[8]{0:T(128)}, u32[]{:S(2)}) %copy-start.12) | copy-done | bytes 56
  9.2 0.0 copy-start.13
  9.2 6.6 %attend.1.part_ref = f32[8,2048]{1,0:T(8,128)S(1)} custom-call(s32[8]{0:T(128)S(1)} %copy-done.12, bf16[8,512]{1,0:T(8,128)(2,1)S(1)} %copy-done.7, bf16[8,512]{1,0:T(8,128)(2,1)S(1)} %copy-done.8, bf16[8,512]{1,0:T(8,128)(2,1)S(1)} %copy-done.9, bf16[8,1024,512]{2,1,0:T(8,128)(2,1)S(1)} %copy-done, bf16[8,1024,512]{2,1,0:T(8,128)(2,1)} %v_hbm.1, ...), custom_call_target="tpu_custom_call" | custom-call | tf_op jit(solution)/shard_map/attend/pallas_call | solution.py:302
  15.8 0.0 copy-done.13
  15.8 0.9 %copy.21.eg_hbm = bf16[1,2048,352]{2,1,0:T(8,128)(2,1)S(1)} copy(bf16[1,2048,352]{1,2,0:T(8,128)(2,1)S(1)} %copy-done.13) | data formatting | bytes 2883584 | tf_op args[13]
  16.7 0.0 copy-start.6
  16.7 0.0 copy-start.10
  16.7 0.0 copy-start.11
  16.7 1.9 %copy.22.eu_hbm = bf16[1,2048,352]{2,1,0:T(8,128)(2,1)S(1)} copy(bf16[1,2048,352]{1,2,0:T(8,128)(2,1)} %param.32) | data formatting | bytes 2883584 | tf_op args[14]
  18.6 0.0 copy-done.6
  18.6 0.0 copy-done.10
  18.6 0.0 copy-done.11
  18.6 0.0 copy-start.2
  18.6 1.4 %copy-done.2 = bf16[1,352,2048]{2,1,0:T(8,128)(2,1)S(1)} copy-done((bf16[1,352,2048]{2,1,0:T(8,128)(2,1)S(1)}, bf16[1,352,2048]{2,1,0:T(8,128)(2,1)}, u32[]{:S(2)}) %copy-start.2) | copy-done | bytes 1441816
  20.0 0.0 copy-start.3
  20.0 1.1 %copy-done.3 = bf16[176,2048]{1,0:T(8,128)(2,1)S(1)} copy-done((bf16[176,2048]{1,0:T(8,128)(2,1)S(1)}, bf16[176,2048]{1,0:T(8,128)(2,1)}, u32[]{:S(2)}) %copy-start.3) | copy-done | bytes 720920
  21.1 0.0 copy-start.4
  21.1 1.1 %copy-done.4 = bf16[176,2048]{1,0:T(8,128)(2,1)S(1)} copy-done((bf16[176,2048]{1,0:T(8,128)(2,1)S(1)}, bf16[176,2048]{1,0:T(8,128)(2,1)}, u32[]{:S(2)}) %copy-start.4) | copy-done | bytes 720920
  22.2 0.0 copy-start.5
  22.2 1.1 %copy-done.5 = bf16[176,2048]{1,0:T(8,128)(2,1)S(1)} copy-done((bf16[176,2048]{1,0:T(8,128)(2,1)S(1)}, bf16[176,2048]{1,0:T(8,128)(2,1)}, u32[]{:S(2)}) %copy-start.5) | copy-done | bytes 720920
  23.3 31.0 %experts.1 = bf16[8,2048]{1,0:T(8,128)(2,1)S(1)} custom-call(f32[8,2048]{1,0:T(8,128)S(1)} %attend.1.part_ref, bf16[8,2048]{1,0:T(8,128)(2,1)S(1)} %copy-done.6, f32[1,2048]{1,0:T(1,128)S(1)} %bitcast.2, f32[1,2048]{1,0:T(1,128)S(1)} %bitcast.3, s32[8,4]{1,0:T(8,128)S(1)} %copy.19.ids_ref, bf16[8,4]{1,0:T(8,128)(2,1)S(1)} %copy.20.rw_ref, ...), custom_call_target="tpu_custom_call" | custom-call | tf_op jit(solution)/shard_map/experts/pallas_call | solution.py:319
  54.3 0.6 %copy.24 = bf16[8,2048]{1,0:T(8,128)(2,1)} copy(bf16[8,2048]{1,0:T(8,128)(2,1)S(1)} %experts.1) | data formatting | bytes 65536
Async XLA Ops:
  1.5 3.4 %copy-start = (bf16[8,1024,512]{2,1,0:T(8,128)(2,1)S(1)}, bf16[8,1024,512]{2,1,0:T(8,128)(2,1)}, u32[]{:S(2)}) copy-start(bf16[8,1024,512]{2,1,0:T(8,128)(2,1)} %k_hbm.1) | copy-start | bytes 25165828
  4.9 1.6 %copy-start.1 = (bf16[512,2048]{1,0:T(8,128)(2,1)S(1)}, bf16[512,2048]{1,0:T(8,128)(2,1)}, u32[]{:S(2)}) copy-start(bf16[512,2048]{1,0:T(8,128)(2,1)} %proj_hbm.1) | copy-start | bytes 6291460
  6.5 0.7 %copy-start.7 = (bf16[8,512]{1,0:T(8,128)(2,1)S(1)}, bf16[8,512]{1,0:T(8,128)(2,1)}, u32[]{:S(2)}) copy-start(bf16[8,512]{1,0:T(8,128)(2,1)} %q_ref.1) | copy-start | bytes 24580
  7.2 0.7 %copy-start.8 = (bf16[8,512]{1,0:T(8,128)(2,1)S(1)}, bf16[8,512]{1,0:T(8,128)(2,1)}, u32[]{:S(2)}) copy-start(bf16[8,512]{1,0:T(8,128)(2,1)} %nk_ref.1) | copy-start | bytes 24580
  7.9 0.7 %copy-start.9 = (bf16[8,512]{1,0:T(8,128)(2,1)S(1)}, bf16[8,512]{1,0:T(8,128)(2,1)}, u32[]{:S(2)}) copy-start(bf16[8,512]{1,0:T(8,128)(2,1)} %nv_ref.1) | copy-start | bytes 24580
  8.6 0.7 %copy-start.12 = (s32[8]{0:T(128)S(1)}, s32[8]{0:T(128)}, u32[]{:S(2)}) copy-start(s32[8]{0:T(128)} %lengths_ref.1) | copy-start | bytes 100
  9.2 6.6 %copy-start.13 = (bf16[1,2048,352]{1,2,0:T(8,128)(2,1)S(1)}, bf16[1,2048,352]{1,2,0:T(8,128)(2,1)}, u32[]{:S(2)}) copy-start(bf16[1,2048,352]{1,2,0:T(8,128)(2,1)} %param.31) | copy-start | bytes 4325380
  16.7 1.9 %copy-start.6 = (bf16[8,2048]{1,0:T(8,128)(2,1)S(1)}, bf16[8,2048]{1,0:T(8,128)(2,1)}, u32[]{:S(2)}) copy-start(bf16[8,2048]{1,0:T(8,128)(2,1)} %hid_ref.1) | copy-start | bytes 98308
  16.7 1.9 %copy-start.10 = (f32[2048]{0:T(1024)S(1)}, f32[2048]{0:T(1024)}, u32[]{:S(2)}) copy-start(f32[2048]{0:T(1024)} %param.26) | copy-start | bytes 24580
  16.7 1.9 %copy-start.11 = (f32[2048]{0:T(1024)S(1)}, f32[2048]{0:T(1024)}, u32[]{:S(2)}) copy-start(f32[2048]{0:T(1024)} %param.30) | copy-start | bytes 24580
  18.6 1.4 %copy-start.2 = (bf16[1,352,2048]{2,1,0:T(8,128)(2,1)S(1)}, bf16[1,352,2048]{2,1,0:T(8,128)(2,1)}, u32[]{:S(2)}) copy-start(bf16[1,352,2048]{2,1,0:T(8,128)(2,1)} %ed_hbm.1) | copy-start | bytes 4325380
  20.0 1.1 %copy-start.3 = (bf16[176,2048]{1,0:T(8,128)(2,1)S(1)}, bf16[176,2048]{1,0:T(8,128)(2,1)}, u32[]{:S(2)}) copy-start(bf16[176,2048]{1,0:T(8,128)(2,1)} %sg_hbm.1) | copy-start | bytes 2162692
  21.1 1.1 %copy-start.4 = (bf16[176,2048]{1,0:T(8,128)(2,1)S(1)}, bf16[176,2048]{1,0:T(8,128)(2,1)}, u32[]{:S(2)}) copy-start(bf16[176,2048]{1,0:T(8,128)(2,1)} %su_hbm.1) | copy-start | bytes 2162692
  22.2 1.1 %copy-start.5 = (bf16[176,2048]{1,0:T(8,128)(2,1)S(1)}, bf16[176,2048]{1,0:T(8,128)(2,1)}, u32[]{:S(2)}) copy-start(bf16[176,2048]{1,0:T(8,128)(2,1)} %sd_hbm.1) | copy-start | bytes 2162692

commit v2 on v1

--- a/solution.py
+++ b/solution.py
@@ -14,9 +14,19 @@
 
 
 def attend_kernel(
-    lengths_ref, q_ref, nk_ref, nv_ref, k_hbm, v_hbm, proj_hbm, out_ref,
-    k_buf, v_buf, proj_buf, attended, k_sem, v_sem, proj_sem,
+    lengths_hbm, q_hbm, nk_hbm, nv_hbm, k_hbm, v_hbm, proj_hbm, out_ref,
+    lengths_ref, q_ref, nk_ref, nv_ref,
+    k_buf, v_buf, proj_buf, attended, k_sem, v_sem, proj_sem, small_sem,
 ):
+    small = [
+        pltpu.make_async_copy(src, dst, small_sem.at[i])
+        for i, (src, dst) in enumerate((
+            (lengths_hbm, lengths_ref), (q_hbm, q_ref), (nk_hbm, nk_ref), (nv_hbm, nv_ref),
+        ))
+    ]
+    for copy in small:
+        copy.start()
+    small[0].wait()
     rows, span, width = k_buf.shape
     heads = width // HD
     chunks = span // CHUNK
@@ -52,6 +62,8 @@
             def _():
                 k_copy(b, c).wait()
 
+    for copy in small[1:]:
+        copy.wait()
     group = max(8, heads)
     row_id = lax.broadcasted_iota(jnp.int32, (group, width), 0)
     lane_head = lax.broadcasted_iota(jnp.int32, (group, width), 1) // HD
@@ -98,9 +110,10 @@
 
 def expert_kernel(
     req_count, head_count,
-    part_ref, hid_ref, gain_ref, score_ref, ids_ref, rw_ref,
+    part_ref, hid_hbm, gain_hbm, score_hbm, ids_hbm, rw_hbm,
     sg_hbm, su_hbm, sd_hbm, eg_hbm, eu_hbm, ed_hbm,
     out_ref,
+    hid_ref, gain_ref, score_ref, ids_ref, rw_ref, small_sems,
     sg, su, sd, eg, eu, ed, weight_sems,
     w_all, terms1, resid_all, send5, terms5, total6, send6, terms6, final,
     w_send, w_recv, s1, r1, s2, r2, s3, r3, s5, r5, s6, r6, s7, r7,
@@ -111,6 +124,15 @@
     me_r = lax.axis_index("req")
     me_h = lax.axis_index("head")
 
+    small = [
+        pltpu.make_async_copy(src, dst, small_sems.at[i])
+        for i, (src, dst) in enumerate((
+            (ids_hbm, ids_ref), (rw_hbm, rw_ref), (hid_hbm, hid_ref), (gain_hbm, gain_ref),
+            (score_hbm, score_ref),
+        ))
+    ]
+    for load in small:
+        load.start()
     loads = [
         pltpu.make_async_copy(src, dst, weight_sems.at[i])
         for i, (src, dst) in enumerate((
@@ -146,10 +168,19 @@
         pl.semaphore_signal(barrier, inc=1, device_id=(req_peer(d), me_h), device_id_type=MESH)
     lane = lax.broadcasted_iota(jnp.int32, (rows, 128), 1)
     table = jnp.zeros((rows, 128), jnp.float32)
+    for load in small:
+        load.wait()
     route = rw_ref[...].astype(jnp.float32)
-    ids = ids_ref[...]
-    for k in range(ids.shape[1]):
-        table = table + jnp.where(ids[:, k:k + 1] == lane, route[:, k:k + 1], 0.0)
+    ids = ids_ref[...].astype(jnp.float32)
+    diagonal = (
+        lax.broadcasted_iota(jnp.int32, (rows, rows), 0)
+        == lax.broadcasted_iota(jnp.int32, (rows, rows), 1)
+    )
+    lane_value = lane.astype(jnp.float32)
+    for k in range(ids.shape[0]):
+        chosen = jnp.sum(jnp.where(diagonal, ids[k:k + 1, :], 0.0), axis=1, keepdims=True)
+        share = jnp.sum(jnp.where(diagonal, route[k:k + 1, :], 0.0), axis=1, keepdims=True)
+        table = table + jnp.where(chosen == lane_value, share, 0.0)
     w_all[me_r] = table
     pl.semaphore_wait(barrier, head_count + req_count - 2)
 
@@ -215,15 +246,6 @@
     for load in loads:
         load.wait()
 
-    def project(weight):
-        out = None
-        for h in range(head_count):
-            term = jnp.dot(
-                normed[h], weight[h * cols:(h + 1) * cols, :], preferred_element_type=jnp.float32
-            )
-            out = term if out is None else out + term
-        return out
-
     def project_t(weight):
         out = None
         for h in range(head_count):
@@ -234,7 +256,7 @@
             out = term if out is None else out + term
         return out
 
-    inner = (silu(project(eg)) * project(eu)).astype(jnp.bfloat16)
+    inner = (silu(project_t(eg)) * project_t(eu)).astype(jnp.bfloat16)
     shared = (silu(project_t(sg)) * project_t(su)).astype(jnp.bfloat16)
     for d in range(1, req_count):
         block = w_all.at[req_source(d)]
@@ -285,7 +307,7 @@
 
 
 VMEM_SPEC = pl.BlockSpec(memory_space=pltpu.VMEM)
-ANY_SPEC = pl.BlockSpec(memory_space=pl.ANY)
+HBM_SPEC = pl.BlockSpec(memory_space=pltpu.HBM)
 
 
 def per_device(
@@ -302,16 +324,20 @@
     partial = pl.pallas_call(
         attend_kernel,
         out_shape=jax.ShapeDtypeStruct((rows, model), f32),
-        in_specs=[pl.BlockSpec(memory_space=pltpu.SMEM)] + [VMEM_SPEC] * 3 + [ANY_SPEC] * 3,
+        in_specs=[HBM_SPEC] * 7,
         out_specs=VMEM_SPEC,
         scratch_shapes=[
+            pltpu.SMEM((rows,), jnp.int32),
+            pltpu.VMEM((rows, width), bf16),
+            pltpu.VMEM((rows, width), bf16),
+            pltpu.VMEM((rows, width), bf16),
             pltpu.VMEM((rows, span, width), bf16),
             pltpu.VMEM((rows, span, width), bf16),
             pltpu.VMEM(out_proj.shape, bf16),
             pltpu.VMEM((rows, width), f32),
-            dma((rows, chunks)), dma((rows, chunks)), dma,
+            dma((rows, chunks)), dma((rows, chunks)), dma, dma((4,)),
         ],
-        compiler_params=pltpu.CompilerParams(vmem_limit_bytes=40 << 20),
+        compiler_params=pltpu.CompilerParams(vmem_limit_bytes=64 << 20),
         name="attend",
     )(lengths, queries, new_keys, new_values, key_cache, value_cache, out_proj)
 
@@ -319,14 +345,20 @@
     return pl.pallas_call(
         functools.partial(expert_kernel, req_count, head_count),
         out_shape=jax.ShapeDtypeStruct((rows, model), bf16),
-        in_specs=[VMEM_SPEC] * 6 + [ANY_SPEC] * 6,
+        in_specs=[VMEM_SPEC] + [HBM_SPEC] * 11,
         out_specs=VMEM_SPEC,
         scratch_shapes=[
+            pltpu.VMEM((rows, model), bf16),
+            pltpu.VMEM((1, model), f32),
+            pltpu.VMEM((1, model), f32),
+            pltpu.VMEM(expert_ids.shape[::-1], jnp.int32),
+            pltpu.VMEM(route_weight.shape[::-1], bf16),
+            dma((5,)),
             pltpu.VMEM(shared_gate.shape, bf16),
             pltpu.VMEM(shared_up.shape, bf16),
             pltpu.VMEM(shared_down.shape, bf16),
-            pltpu.VMEM(expert_gate.shape[1:], bf16),
-            pltpu.VMEM(expert_up.shape[1:], bf16),
+            pltpu.VMEM(expert_gate.shape[:0:-1], bf16),
+            pltpu.VMEM(expert_up.shape[:0:-1], bf16),
             pltpu.VMEM(expert_down.shape[1:], bf16),
             dma((6,)),
             pltpu.VMEM((req_count, rows, 128), f32),
@@ -347,13 +379,14 @@
             dma((head_count,)), dma((head_count,)),
         ],
         compiler_params=pltpu.CompilerParams(
-            vmem_limit_bytes=40 << 20, collective_id=0, has_side_effects=True
+            vmem_limit_bytes=64 << 20, collective_id=0, has_side_effects=True
         ),
         name="experts",
     )(
         partial, hidden_in, norm_gain.reshape(1, model), shared_score.reshape(1, model),
-        expert_ids, route_weight,
-        shared_gate, shared_up, shared_down, expert_gate, expert_up, expert_down,
+        expert_ids.T, route_weight.T,
+        shared_gate, shared_up, shared_down,
+        jnp.swapaxes(expert_gate, 1, 2), jnp.swapaxes(expert_up, 1, 2), expert_down,
     )
 
 

time: 55.4 us -> 42.2 us (0.76)
  local copies, waits for them, and re-layouts: 17.3 us -> 1.38 us
  Pallas kernels: 37.5 us -> 40.4 us
    unnamed x33 -> x1, local copies, waits for them, and re-layouts: 17.3 us -> 1.38 us
    pallas_call x1, Pallas kernels: 6.55 us -> 9.07 us  [per_device(): pl.pallas_call(attend_kernel, out_shape=jax.ShapeDtypeStruct((rows, model...]
where the time goes in v2:
time: 42.2 us; the launch traced here: 41.7 us
  Pallas kernels  40.4 us (96%)
  local copies, waits for them, and re-layouts  1.38 us (3%)
    pallas_call x1, Pallas kernels, per_device(): pl.pallas_call(functools.partial(expert_kernel, req_count, head_count), o...  31.3 us
    pallas_call x1, Pallas kernels, per_device(): pl.pallas_call(attend_kernel, out_shape=jax.ShapeDtypeStruct((rows, model...  9.07 us
    unnamed x1, local copies, waits for them, and re-layouts  1.38 us

profile of v2, /device:TPU:0, one launch (start us, length us, event | category | flops | bytes accessed | tf_op | source)
XLA Modules:
  0.0 41.7 jit_solution(16647047251638123440)
XLA Ops:
  0.0 9.1 %attend.1.part_ref = f32[8,2048]{1,0:T(8,128)} custom-call(s32[8]{0:T(128)} %lengths_hbm.1, bf16[8,512]{1,0:T(8,128)(2,1)} %q_hbm.1, bf16[8,512]{1,0:T(8,128)(2,1)} %nk_hbm.1, bf16[8,512]{1,0:T(8,128)(2,1)} %nv_hbm.1, bf16[8,1024,512]{2,1,0:T(8,128)(2,1)} %k_hbm.1, bf16[8,1024,512]{2,1,0:T(8,128)(2,1)} %v_hbm.1, bf16[512,2048]{1,0:T(8,128)(2,1)} %proj_hbm.1), custom_call_target="tpu_custom_call" | custom-call | tf_op jit(solution)/shard_map/attend/pallas_call | solution.py:324
  9.1 31.3 %experts.1 = bf16[8,2048]{1,0:T(8,128)(2,1)} custom-call(f32[8,2048]{1,0:T(8,128)} %attend.1.part_ref, bf16[8,2048]{1,0:T(8,128)(2,1)} %hid_hbm.1, f32[1,2048]{1,0:T(1,128)} %bitcast.8, f32[1,2048]{1,0:T(1,128)} %bitcast.9, s32[4,8]{1,0:T(4,128)} %bitcast.10, bf16[4,8]{1,0:T(4,128)(2,1)} %bitcast.11, bf16[176,2048]{1,0:T(8,128)(2,1)} %sg_hbm.1, ...), custom_call_target="tpu_custom_call" | custom-call | tf_op jit(solution)/shard_map/experts/pallas_call | solution.py:345
  40.4 1.4 %copy.20 = bf16[8,2048]{1,0:T(8,128)(2,1)} copy(bf16[8,2048]{1,0:T(8,128)(2,1)} %experts.1) | data formatting | bytes 65536

commit v3 on v2

--- a/solution.py
+++ b/solution.py
@@ -9,110 +9,21 @@
 
 HD = 128
 EPSILON = 1e-06
-CHUNK = 256
 MESH = pl.DeviceIdType.MESH
-
-
-def attend_kernel(
-    lengths_hbm, q_hbm, nk_hbm, nv_hbm, k_hbm, v_hbm, proj_hbm, out_ref,
-    lengths_ref, q_ref, nk_ref, nv_ref,
-    k_buf, v_buf, proj_buf, attended, k_sem, v_sem, proj_sem, small_sem,
-):
-    small = [
-        pltpu.make_async_copy(src, dst, small_sem.at[i])
-        for i, (src, dst) in enumerate((
-            (lengths_hbm, lengths_ref), (q_hbm, q_ref), (nk_hbm, nk_ref), (nv_hbm, nv_ref),
-        ))
-    ]
-    for copy in small:
-        copy.start()
-    small[0].wait()
-    rows, span, width = k_buf.shape
-    heads = width // HD
-    chunks = span // CHUNK
-    scale = HD ** (-0.5)
-
-    def k_copy(b, c):
-        part = pl.ds(c * CHUNK, CHUNK)
-        return pltpu.make_async_copy(k_hbm.at[b, part], k_buf.at[b, part], k_sem.at[b, c])
-
-    def v_copy(b, c):
-        part = pl.ds(c * CHUNK, CHUNK)
-        return pltpu.make_async_copy(v_hbm.at[b, part], v_buf.at[b, part], v_sem.at[b, c])
-
-    def live(b, c):
-        return lengths_ref[b] > c * CHUNK
-
-    for copy in (k_copy, v_copy):
-        for b in range(rows):
-            for c in range(chunks):
-                @pl.when(live(b, c))
-                def _():
-                    copy(b, c).start()
-    proj_copy = pltpu.make_async_copy(proj_hbm, proj_buf, proj_sem)
-    proj_copy.start()
-    for b in range(rows):
-        for c in range(1, chunks):
-            @pl.when(jnp.logical_not(live(b, c)))
-            def _():
-                v_buf[b, c * CHUNK:(c + 1) * CHUNK, :] = jnp.zeros((CHUNK, width), v_buf.dtype)
-    for b in range(rows):
-        for c in range(chunks):
-            @pl.when(live(b, c))
-            def _():
-                k_copy(b, c).wait()
-
-    for copy in small[1:]:
-        copy.wait()
-    group = max(8, heads)
-    row_id = lax.broadcasted_iota(jnp.int32, (group, width), 0)
-    lane_head = lax.broadcasted_iota(jnp.int32, (group, width), 1) // HD
-    own_head = row_id == lane_head
-    position = lax.broadcasted_iota(jnp.int32, (group, span), 1)
-    queries = q_ref[...].astype(jnp.float32)
-    own_keys = nk_ref[...].astype(jnp.float32)
-    own_values = nv_ref[...].astype(jnp.float32)
-    probs = []
-    own_probs = []
-    for b in range(rows):
-        spread = jnp.where(own_head, queries[b:b + 1, :], 0.0)
-        scores = lax.dot_general(
-            spread.astype(jnp.bfloat16), k_buf[b], (((1,), (1,)), ((), ())),
-            preferred_element_type=jnp.float32,
-        ) * scale
-        own_score = jnp.sum(spread * own_keys[b:b + 1, :], axis=1, keepdims=True) * scale
-        alive = position < lengths_ref[b]
-        scores = jnp.where(alive, scores, -1e30)
-        highest = jnp.maximum(jnp.max(scores, axis=1, keepdims=True), own_score)
-        weights = jnp.where(alive, jnp.exp(scores - highest), 0.0)
-        own_weight = jnp.exp(own_score - highest)
-        total = jnp.sum(weights, axis=1, keepdims=True) + own_weight
-        probs.append((weights / total).astype(jnp.bfloat16))
-        own_probs.append((own_weight / total).astype(jnp.bfloat16).astype(jnp.float32))
-    for b in range(rows):
-        for c in range(chunks):
-            @pl.when(live(b, c))
-            def _():
-                v_copy(b, c).wait()
-    for b in range(rows):
-        mixed = jnp.dot(probs[b], v_buf[b], preferred_element_type=jnp.float32)
-        mixed = mixed + own_probs[b] * own_values[b:b + 1, :]
-        attended[b:b + 1, :] = jnp.sum(jnp.where(own_head, mixed, 0.0), axis=0, keepdims=True)
-    proj_copy.wait()
-    out_ref[...] = jnp.dot(
-        attended[...].astype(jnp.bfloat16), proj_buf[...], preferred_element_type=jnp.float32
-    )
 
 
 def silu(x):
     return x / (1.0 + jnp.exp(-x))
 
 
-def expert_kernel(
+def layer_kernel(
     req_count, head_count,
-    part_ref, hid_hbm, gain_hbm, score_hbm, ids_hbm, rw_hbm,
+    lengths_hbm, q_hbm, nk_hbm, nv_hbm, k_hbm, v_hbm, proj_hbm,
+    hid_hbm, gain_hbm, score_hbm, ids_hbm, rw_hbm,
     sg_hbm, su_hbm, sd_hbm, eg_hbm, eu_hbm, ed_hbm,
     out_ref,
+    lengths_ref, q_ref, nk_ref, nv_ref, k_buf, v_buf, proj_buf, k_sem, v_sem, proj_sem,
+    attended, part_ref,
     hid_ref, gain_ref, score_ref, ids_ref, rw_ref, small_sems,
     sg, su, sd, eg, eu, ed, weight_sems,
     w_all, terms1, resid_all, send5, terms5, total6, send6, terms6, final,
@@ -124,15 +35,48 @@
     me_r = lax.axis_index("req")
     me_h = lax.axis_index("head")
 
+    def req_peer(d):
+        return lax.rem(me_r + d, req_count)
+
+    def req_source(d):
+        return lax.rem(me_r + (req_count - d), req_count)
+
+    def head_peer(d):
+        return lax.rem(me_h + d, head_count)
+
+    def head_source(d):
+        return lax.rem(me_h + (head_count - d), head_count)
+
+    def remote(src, dst, send, recv, r, h):
+        return pltpu.make_async_remote_copy(
+            src_ref=src, dst_ref=dst, send_sem=send, recv_sem=recv,
+            device_id=(r, h), device_id_type=MESH,
+        )
+
+    barrier = pltpu.get_barrier_semaphore()
+    for d in range(1, head_count):
+        pl.semaphore_signal(barrier, inc=1, device_id=(me_r, head_peer(d)), device_id_type=MESH)
+    for d in range(1, req_count):
+        pl.semaphore_signal(barrier, inc=1, device_id=(req_peer(d), me_h), device_id_type=MESH)
     small = [
         pltpu.make_async_copy(src, dst, small_sems.at[i])
         for i, (src, dst) in enumerate((
+            (lengths_hbm, lengths_ref), (q_hbm, q_ref), (nk_hbm, nk_ref), (nv_hbm, nv_ref),
             (ids_hbm, ids_ref), (rw_hbm, rw_ref), (hid_hbm, hid_ref), (gain_hbm, gain_ref),
             (score_hbm, score_ref),
         ))
     ]
     for load in small:
         load.start()
+    caches = [
+        [pltpu.make_async_copy(hbm.at[b], buf.at[b], sem.at[b]) for b in range(rows)]
+        for hbm, buf, sem in ((k_hbm, k_buf, k_sem), (v_hbm, v_buf, v_sem))
+    ]
+    for loads in caches:
+        for load in loads:
+            load.start()
+    proj_load = pltpu.make_async_copy(proj_hbm, proj_buf, proj_sem)
+    proj_load.start()
     loads = [
         pltpu.make_async_copy(src, dst, weight_sems.at[i])
         for i, (src, dst) in enumerate((
@@ -143,33 +87,43 @@
     for load in loads:
         load.start()
 
-    def req_peer(d):
-        return lax.rem(me_r + d, req_count)
-
-    def req_source(d):
-        return lax.rem(me_r + (req_count - d), req_count)
-
-    def head_peer(d):
-        return lax.rem(me_h + d, head_count)
-
-    def head_source(d):
-        return lax.rem(me_h + (head_count - d), head_count)
-
-    def remote(src, dst, send, recv, r, h):
-        return pltpu.make_async_remote_copy(
-            src_ref=src, dst_ref=dst, send_sem=send, recv_sem=recv,
-            device_id=(r, h), device_id_type=MESH,
-        )
-
-    barrier = pltpu.get_barrier_semaphore()
-    for d in range(1, head_count):
-        pl.semaphore_signal(barrier, inc=1, device_id=(me_r, head_peer(d)), device_id_type=MESH)
-    for d in range(1, req_count):
-        pl.semaphore_signal(barrier, inc=1, device_id=(req_peer(d), me_h), device_id_type=MESH)
+    for load in small:
+        load.wait()
+
+    span, width = k_buf.shape[1:]
+    scale = HD ** (-0.5)
+    group = max(8, width // HD)
+    own_head = (
+        lax.broadcasted_iota(jnp.int32, (group, width), 0)
+        == lax.broadcasted_iota(jnp.int32, (group, width), 1) // HD
+    )
+    position = lax.broadcasted_iota(jnp.int32, (group, span), 1)
+    queries = q_ref[...].astype(jnp.float32)
+    own_keys = nk_ref[...].astype(jnp.float32)
+    own_values = nv_ref[...].astype(jnp.float32)
+    spread = [jnp.where(own_head, queries[b:b + 1, :], 0.0) for b in range(rows)]
+    all_scores = []
+    for b in range(rows):
+        caches[0][b].wait()
+        all_scores.append(lax.dot_general(
+            spread[b].astype(jnp.bfloat16), k_buf[b], (((1,), (1,)), ((), ())),
+            preferred_element_type=jnp.float32,
+        ))
+    probs = []
+    own_probs = []
+    for b in range(rows):
+        own_score = jnp.sum(spread[b] * own_keys[b:b + 1, :], axis=1, keepdims=True) * scale
+        alive = position < lengths_ref[b]
+        scores = jnp.where(alive, all_scores[b] * scale, -1e30)
+        highest = jnp.maximum(jnp.max(scores, axis=1, keepdims=True), own_score)
+        exps = jnp.where(alive, jnp.exp(scores - highest), 0.0)
+        own_exp = jnp.exp(own_score - highest)
+        norm = jnp.sum(exps, axis=1, keepdims=True) + own_exp
+        probs.append((exps / norm).astype(jnp.bfloat16))
+        own_probs.append((own_exp / norm).astype(jnp.bfloat16).astype(jnp.float32))
+
     lane = lax.broadcasted_iota(jnp.int32, (rows, 128), 1)
     table = jnp.zeros((rows, 128), jnp.float32)
-    for load in small:
-        load.wait()
     route = rw_ref[...].astype(jnp.float32)
     ids = ids_ref[...].astype(jnp.float32)
     diagonal = (
@@ -193,14 +147,23 @@
         copy.start()
         sends.append(copy)
 
+    for d in range(1, req_count):
+        start(remote(
+            w_all.at[me_r], w_all.at[me_r], w_send.at[d], w_recv.at[d], req_peer(d), me_h,
+        ))
+    for b in range(rows):
+        caches[1][b].wait()
+        mixed = jnp.dot(probs[b], v_buf[b], preferred_element_type=jnp.float32)
+        mixed = mixed + own_probs[b] * own_values[b:b + 1, :]
+        attended[b:b + 1, :] = jnp.sum(jnp.where(own_head, mixed, 0.0), axis=0, keepdims=True)
+    proj_load.wait()
+    part_ref[...] = jnp.dot(
+        attended[...].astype(jnp.bfloat16), proj_buf[...], preferred_element_type=jnp.float32
+    )
     for d in range(1, head_count):
         start(remote(
             part_ref.at[:, my_cols(head_peer(d))], terms1.at[d], s1.at[d], r1.at[d],
             me_r, head_peer(d),
-        ))
-    for d in range(1, req_count):
-        start(remote(
-            w_all.at[me_r], w_all.at[me_r], w_send.at[d], w_recv.at[d], req_peer(d), me_h,
         ))
     summed = part_ref[:, my_cols(me_h)]
     for d in range(1, head_count):
@@ -320,11 +283,11 @@
     span, width = key_cache.shape[1:]
     bf16, f32 = jnp.bfloat16, jnp.float32
     dma = pltpu.SemaphoreType.DMA
-    chunks = span // CHUNK
-    partial = pl.pallas_call(
-        attend_kernel,
-        out_shape=jax.ShapeDtypeStruct((rows, model), f32),
-        in_specs=[HBM_SPEC] * 7,
+    cols = model // head_count
+    return pl.pallas_call(
+        functools.partial(layer_kernel, req_count, head_count),
+        out_shape=jax.ShapeDtypeStruct((rows, model), bf16),
+        in_specs=[HBM_SPEC] * 18,
         out_specs=VMEM_SPEC,
         scratch_shapes=[
             pltpu.SMEM((rows,), jnp.int32),
@@ -334,26 +297,15 @@
             pltpu.VMEM((rows, span, width), bf16),
             pltpu.VMEM((rows, span, width), bf16),
             pltpu.VMEM(out_proj.shape, bf16),
+            dma((rows,)), dma((rows,)), dma,
             pltpu.VMEM((rows, width), f32),
-            dma((rows, chunks)), dma((rows, chunks)), dma, dma((4,)),
-        ],
-        compiler_params=pltpu.CompilerParams(vmem_limit_bytes=64 << 20),
-        name="attend",
-    )(lengths, queries, new_keys, new_values, key_cache, value_cache, out_proj)
-
-    cols = model // head_count
-    return pl.pallas_call(
-        functools.partial(expert_kernel, req_count, head_count),
-        out_shape=jax.ShapeDtypeStruct((rows, model), bf16),
-        in_specs=[VMEM_SPEC] + [HBM_SPEC] * 11,
-        out_specs=VMEM_SPEC,
-        scratch_shapes=[
+            pltpu.VMEM((rows, model), f32),
             pltpu.VMEM((rows, model), bf16),
             pltpu.VMEM((1, model), f32),
             pltpu.VMEM((1, model), f32),
             pltpu.VMEM(expert_ids.shape[::-1], jnp.int32),
             pltpu.VMEM(route_weight.shape[::-1], bf16),
-            dma((5,)),
+            dma((9,)),
             pltpu.VMEM(shared_gate.shape, bf16),
             pltpu.VMEM(shared_up.shape, bf16),
             pltpu.VMEM(shared_down.shape, bf16),
@@ -381,9 +333,10 @@
         compiler_params=pltpu.CompilerParams(
             vmem_limit_bytes=64 << 20, collective_id=0, has_side_effects=True
         ),
-        name="experts",
+        name="layer",
     )(
-        partial, hidden_in, norm_gain.reshape(1, model), shared_score.reshape(1, model),
+        lengths, queries, new_keys, new_values, key_cache, value_cache, out_proj,
+        hidden_in, norm_gain.reshape(1, model), shared_score.reshape(1, model),
         expert_ids.T, route_weight.T,
         shared_gate, shared_up, shared_down,
         jnp.swapaxes(expert_gate, 1, 2), jnp.swapaxes(expert_up, 1, 2), expert_down,

time: 42.2 us -> 41.9 us (level)
    pallas_call x2 -> x1, Pallas kernels: 40.4 us -> 40.4 us  [per_device(): pl.pallas_call(functools.partial(layer_kernel, req_count, head_count), ou...]
where the time goes in v3:
time: 41.9 us; the launch traced here: 41.7 us
  Pallas kernels  40.4 us (96%)
  local copies, waits for them, and re-layouts  1.38 us (3%)
    pallas_call x1, Pallas kernels, per_device(): pl.pallas_call(functools.partial(layer_kernel, req_count, head_count), ou...  40.4 us
    unnamed x1, local copies, waits for them, and re-layouts  1.38 us

profile of v3, /device:TPU:0, one launch (start us, length us, event | category | flops | bytes accessed | tf_op | source)
XLA Modules:
  0.0 41.7 jit_solution(5508160787662341042)
XLA Ops:
  0.0 40.4 %layer.1 = bf16[8,2048]{1,0:T(8,128)(2,1)} custom-call(s32[8]{0:T(128)} %lengths_hbm.1, bf16[8,512]{1,0:T(8,128)(2,1)} %q_hbm.1, bf16[8,512]{1,0:T(8,128)(2,1)} %nk_hbm.1, bf16[8,512]{1,0:T(8,128)(2,1)} %nv_hbm.1, bf16[8,1024,512]{2,1,0:T(8,128)(2,1)} %k_hbm.1, bf16[8,1024,512]{2,1,0:T(8,128)(2,1)} %v_hbm.1, bf16[512,2048]{1,0:T(8,128)(2,1)} %proj_hbm.1, ...), custom_call_target="tpu_custom_call" | custom-call | tf_op jit(solution)/shard_map/layer/pallas_call | solution.py:287
  40.4 1.4 %copy.20 = bf16[8,2048]{1,0:T(8,128)(2,1)} copy(bf16[8,2048]{1,0:T(8,128)(2,1)} %layer.1) | data formatting | bytes 65536

commit v4 on v3

--- a/solution.py
+++ b/solution.py
@@ -72,11 +72,9 @@
         [pltpu.make_async_copy(hbm.at[b], buf.at[b], sem.at[b]) for b in range(rows)]
         for hbm, buf, sem in ((k_hbm, k_buf, k_sem), (v_hbm, v_buf, v_sem))
     ]
-    for loads in caches:
-        for load in loads:
-            load.start()
+    for load in caches[0]:
+        load.start()
     proj_load = pltpu.make_async_copy(proj_hbm, proj_buf, proj_sem)
-    proj_load.start()
     loads = [
         pltpu.make_async_copy(src, dst, weight_sems.at[i])
         for i, (src, dst) in enumerate((
@@ -84,8 +82,6 @@
             (sd_hbm, sd), (ed_hbm.at[0], ed),
         ))
     ]
-    for load in loads:
-        load.start()
 
     for load in small:
         load.wait()
@@ -105,10 +101,12 @@
     all_scores = []
     for b in range(rows):
         caches[0][b].wait()
+        caches[1][b].start()
         all_scores.append(lax.dot_general(
             spread[b].astype(jnp.bfloat16), k_buf[b], (((1,), (1,)), ((), ())),
             preferred_element_type=jnp.float32,
         ))
+    proj_load.start()
     probs = []
     own_probs = []
     for b in range(rows):
@@ -165,6 +163,8 @@
             part_ref.at[:, my_cols(head_peer(d))], terms1.at[d], s1.at[d], r1.at[d],
             me_r, head_peer(d),
         ))
+    for load in loads:
+        load.start()
     summed = part_ref[:, my_cols(me_h)]
     for d in range(1, head_count):
         remote(

time: 41.9 us -> 38.1 us (0.909)
  Pallas kernels: 40.4 us -> 36.5 us
    pallas_call x1, Pallas kernels: 40.4 us -> 36.5 us  [per_device(): pl.pallas_call(functools.partial(layer_kernel, req_count, head_count), ou...]
where the time goes in v4:
time: 38.1 us; the launch traced here: 37.9 us
  Pallas kernels  36.5 us (96%)
  local copies, waits for them, and re-layouts  1.38 us (4%)
    pallas_call x1, Pallas kernels, per_device(): pl.pallas_call(functools.partial(layer_kernel, req_count, head_count), ou...  36.5 us
    unnamed x1, local copies, waits for them, and re-layouts  1.38 us

profile of v4, /device:TPU:0, one launch (start us, length us, event | category | flops | bytes accessed | tf_op | source)
XLA Modules:
  0.0 37.9 jit_solution(11256921209579483771)
XLA Ops:
  0.0 36.5 %layer.1 = bf16[8,2048]{1,0:T(8,128)(2,1)} custom-call(s32[8]{0:T(128)} %lengths_hbm.1, bf16[8,512]{1,0:T(8,128)(2,1)} %q_hbm.1, bf16[8,512]{1,0:T(8,128)(2,1)} %nk_hbm.1, bf16[8,512]{1,0:T(8,128)(2,1)} %nv_hbm.1, bf16[8,1024,512]{2,1,0:T(8,128)(2,1)} %k_hbm.1, bf16[8,1024,512]{2,1,0:T(8,128)(2,1)} %v_hbm.1, bf16[512,2048]{1,0:T(8,128)(2,1)} %proj_hbm.1, ...), custom_call_target="tpu_custom_call" | custom-call | tf_op jit(solution)/shard_map/layer/pallas_call | solution.py:287
  36.6 1.4 %copy.20 = bf16[8,2048]{1,0:T(8,128)(2,1)} copy(bf16[8,2048]{1,0:T(8,128)(2,1)} %layer.1) | data formatting | bytes 65536
